TPU v7x, 128 devices: a whole 4x4x4 slice. The times are simulated.
128 devices in a mesh: req: 8 (over z, core), exp: 16 (over y, x).
Axes of the slice: x: 4, y: 4, z: 4, core: 2. Of those that a mesh axis runs over, the one named last changes fastest.
Arguments:
- hidden: bfloat16 [16384, 2048], P(('req', 'exp')), may hold values from -6 to 6
- attn_gain: float32 [2048], replicated, may hold values from 0.5 to 1.5
- w_query: bfloat16 [2048, 2048], P(None, 'exp'), may hold values from -0.125 to 0.125
- w_keyval: bfloat16 [2, 2048, 2048], P(None, None, 'exp'), may hold values from -0.3125 to 0.3125
- k_pool: bfloat16 [1280, 128, 2048], P('req', None, 'exp'), may hold values from -86 to 86
- v_pool: bfloat16 [1280, 128, 2048], P('req', None, 'exp'), may hold values from -16 to 16
- dec_len: int32 [32], P('req'), may hold values from 1 to 4096, as said below
- dec_pages: int32 [32, 32], P('req'), may hold values from 0 to 159, as said below
- pre_pos: int32 [8], P('req'), may hold values from 0 to 4096, as said below
- pre_pages: int32 [8, 32], P('req'), may hold values from 0 to 159
- w_out: bfloat16 [2048, 2048], P('exp'), may hold values from -0.125 to 0.125
- moe_gain: float32 [2048], replicated, may hold values from 0.1 to 1.9
- expert_ids: int32 [16384, 8], P(('req', 'exp')), may hold values from 0 to 63, all different within a row; in each aligned block of 128 rows (0 to 127, 128 to 255, ...) at most 20 rows name the same one
- router_logits: float32 [16384, 8], P(('req', 'exp')), may hold values from -0.4 to 283
- w_in: bfloat16 [128, 2048, 1024], P(('req', 'exp')), may hold values from -0.125 to 0.125
- w_down: bfloat16 [128, 512, 2048], P(('req', 'exp')), may hold values from -0.25 to 0.25
Outputs:
- mixed: bfloat16 [16384, 2048], P(('req', 'exp'))
- new_kv: bfloat16 [2, 16384, 2048], P(None, 'req', 'exp')
Inputs may be any that keep to these rules, and one draw needn't show every extreme that they name: Within each group, the rows of dec_pages of its 4 requests and its row of pre_pages name every one of the group's 160 pages exactly once. `dec_len`: some request has exactly 4096 cached positions. `pre_pos`: some group's prefix has exactly 4096 positions. `expert_ids`: each row names 8 different experts; among the rows of one device no expert is named by more than 20 rows.
All inputs are finite; a program needn't handle non-finite values.
Results may differ from a plain program's by a relative error of at most 0.02.
Values may be sent and summed in bfloat16 or wider, within the bound.
A program may use at most 128 MiB of HBM per device.

v0:
```python
import math

import jax
import jax.numpy as jnp
from jax import lax
from jax.sharding import PartitionSpec as P

HD = 128
SPLIT = 2


EPSILON = 1e-05
THETA = 10000.0


def rms_scale(inputs, gain):
    values = inputs.astype(jnp.float32)
    mean_square = jnp.mean(values * values, axis=-1, keepdims=True)
    return (values * lax.rsqrt(mean_square + EPSILON) * gain).astype(jnp.bfloat16)


def rotate(values, positions):
    head_size = values.shape[-1]
    half = head_size // 2
    steps = jnp.arange(half, dtype=jnp.float32)
    frequency = jnp.exp(steps * (-2.0 * math.log(THETA) / head_size))
    angles = positions.astype(jnp.float32)[:, None, None] * frequency[None, None, :]
    cosine = jnp.cos(angles)
    sine = jnp.sin(angles)
    first = values[..., :half]
    second = values[..., half:]
    return jnp.concatenate(
        [first * cosine - second * sine, second * cosine + first * sine], axis=-1
    )


def online_block(state, query, keys, values, allowed, scale):
    old_max, old_total, running = state
    scores = jnp.einsum("qd,kd->qk", query, keys, preferred_element_type=jnp.float32) * scale
    scores = jnp.where(allowed, scores, -jnp.inf)
    new_max = jnp.maximum(old_max, jnp.max(scores, axis=1))
    anchor = jnp.where(jnp.isfinite(new_max), new_max, 0.0)
    shrink = jnp.exp(old_max - anchor)
    weights = jnp.exp(scores - anchor[:, None])
    new_total = old_total * shrink + jnp.sum(weights, axis=1)
    running = running * shrink[:, None] + jnp.dot(
        weights.astype(jnp.bfloat16), values, preferred_element_type=jnp.float32
    )
    return (new_max, new_total, running)


def deliver(buffer):
    result = lax.all_to_all(buffer, ("req", "exp"), split_axis=0, concat_axis=0, tiled=True)
    return result


def bring_back(buffer):
    result = lax.all_to_all(buffer, ("req", "exp"), split_axis=0, concat_axis=0, tiled=True)
    return result


def body(
    hidden,
    attn_gain,
    w_query,
    w_keyval,
    k_pool,
    v_pool,
    dec_len,
    dec_pages,
    pre_pos,
    pre_pages,
    w_out,
    moe_gain,
    expert_ids,
    router_logits,
    w_in,
    w_down,
):
    local_rows, width = hidden.shape
    req_count = lax.axis_size("req")
    exp_count = lax.axis_size("exp")
    devices = req_count * exp_count
    group_rows = local_rows * exp_count
    dec_count = dec_len.shape[0]
    segment = group_rows - dec_count
    local_width = w_query.shape[1]
    heads_here = local_width // HD
    page_size = k_pool.shape[1]
    scale = 1.0 / math.sqrt(HD)
    normed_attn = rms_scale(hidden, attn_gain)
    joined = jnp.concatenate([w_query, w_keyval[0], w_keyval[1]], axis=1)
    projected_rows = jnp.dot(
        lax.all_gather(normed_attn, "exp", axis=0, tiled=True),
        joined,
        preferred_element_type=jnp.float32,
    )
    row_index = jnp.arange(group_rows, dtype=jnp.int32)
    dec_index = jnp.minimum(row_index, dec_count - 1)
    positions = jnp.where(
        row_index < dec_count, dec_len[dec_index], pre_pos[0] + row_index - dec_count
    )
    query = rotate(
        projected_rows[:, :local_width].reshape(group_rows, heads_here, HD), positions
    ).astype(jnp.bfloat16)
    keys_new = rotate(
        projected_rows[:, local_width : 2 * local_width].reshape(group_rows, heads_here, HD),
        positions,
    ).astype(jnp.bfloat16)
    values_new = (
        projected_rows[:, 2 * local_width :]
        .reshape(group_rows, heads_here, HD)
        .astype(jnp.bfloat16)
    )
    new_kv = jnp.stack(
        [keys_new.reshape(group_rows, local_width), values_new.reshape(group_rows, local_width)]
    )
    cache_len = dec_pages.shape[1] * page_size
    table_keys = k_pool[dec_pages].reshape(dec_count, cache_len, heads_here, HD)
    table_values = v_pool[dec_pages].reshape(dec_count, cache_len, heads_here, HD)
    dec_query = query[:dec_count]
    dec_scores = (
        jnp.einsum("rhd,rkhd->rhk", dec_query, table_keys, preferred_element_type=jnp.float32)
        * scale
    )
    own_score = (
        jnp.einsum(
            "rhd,rhd->rh", dec_query, keys_new[:dec_count], preferred_element_type=jnp.float32
        )
        * scale
    )
    visible = (jnp.arange(cache_len, dtype=jnp.int32)[None, :] < dec_len[:, None])[:, None, :]
    dec_scores = jnp.where(visible, dec_scores, -jnp.inf)
    highest = jnp.maximum(jnp.max(dec_scores, axis=2), own_score)
    dec_weights = jnp.exp(dec_scores - highest[..., None])
    own_weight = jnp.exp(own_score - highest)
    dec_total = jnp.sum(dec_weights, axis=2) + own_weight
    own_rounded = lax.optimization_barrier(own_weight.astype(jnp.bfloat16)).astype(jnp.float32)
    dec_summed = jnp.einsum(
        "rhk,rkhd->rhd",
        dec_weights.astype(jnp.bfloat16),
        table_values,
        preferred_element_type=jnp.float32,
    )
    dec_summed = dec_summed + own_rounded[..., None] * values_new[:dec_count].astype(jnp.float32)
    dec_out = (
        (dec_summed / dec_total[..., None]).astype(jnp.bfloat16).reshape(dec_count, local_width)
    )
    prefix_count = pre_pages.shape[1]
    block_pages = math.gcd(prefix_count, max(1, 512 // page_size))
    block_keys = block_pages * page_size
    block_count = prefix_count // block_pages
    length = pre_pos[0]
    order = jnp.arange(segment, dtype=jnp.int32)
    causal = order[None, :] <= order[:, None]
    seg_query = query[dec_count:, 0]

    def prefix_step(block, state):
        chosen = lax.dynamic_slice_in_dim(pre_pages[0], block * block_pages, block_pages)
        block_k = k_pool[chosen].reshape(block_keys, HD)
        block_v = v_pool[chosen].reshape(block_keys, HD)
        slots = block * block_keys + jnp.arange(block_keys, dtype=jnp.int32)
        return online_block(state, seg_query, block_k, block_v, (slots < length)[None, :], scale)

    start_state = (
        jnp.full((segment,), -jnp.inf, jnp.float32),
        jnp.zeros((segment,), jnp.float32),
        jnp.zeros((segment, HD), jnp.float32),
    )
    state = lax.fori_loop(0, block_count, prefix_step, start_state)
    state = online_block(
        state, seg_query, keys_new[dec_count:, 0], values_new[dec_count:, 0], causal, scale
    )
    head_outputs = (state[2] / state[1][:, None]).astype(jnp.bfloat16)
    attended = jnp.concatenate([dec_out, head_outputs], axis=0)
    projected = lax.psum_scatter(
        jnp.dot(attended, w_out, preferred_element_type=jnp.float32).astype(jnp.bfloat16),
        "exp",
        scatter_dimension=0,
        tiled=True,
    ).astype(jnp.float32)
    residual = (hidden.astype(jnp.float32) + projected).astype(jnp.bfloat16)
    normed_moe = rms_scale(residual, moe_gain)
    gates = jax.nn.softmax(router_logits, axis=-1)
    experts = devices // SPLIT
    top = expert_ids.shape[1]
    capacity = 2 * ((local_rows * top * 5 + 8 * experts - 1) // (8 * experts))
    assigned = expert_ids.reshape(-1)
    count_all = assigned.shape[0]
    marks = (assigned[:, None] == jnp.arange(experts, dtype=jnp.int32)[None, :]).astype(jnp.int32)
    earlier = jnp.cumsum(marks, axis=0) - marks
    place = jnp.sum(earlier * marks, axis=1)
    target = assigned * capacity + place
    owner_rows = jnp.arange(count_all, dtype=jnp.int32) // top
    outgoing = (
        jnp.zeros((experts * capacity, width), jnp.bfloat16).at[target].set(normed_moe[owner_rows])
    )
    doubled = jnp.broadcast_to(
        outgoing.reshape(experts, 1, capacity, width), (experts, SPLIT, capacity, width)
    ).reshape(devices, capacity, width)
    arrived = deliver(doubled)
    piece_units = w_down.shape[1]
    inner = jnp.dot(
        arrived.reshape(devices * capacity, width), w_in[0], preferred_element_type=jnp.float32
    )
    activated = (jax.nn.silu(inner[:, :piece_units]) * inner[:, piece_units:]).astype(jnp.bfloat16)
    partial_value = (
        jnp.dot(activated, w_down[0], preferred_element_type=jnp.float32)
        .astype(jnp.bfloat16)
        .reshape(devices, capacity, width)
    )
    returned = bring_back(partial_value).reshape(devices * capacity, width)
    base_index = assigned * (SPLIT * capacity) + place
    lower_half = returned[base_index].astype(jnp.float32)
    upper_half = returned[base_index + capacity].astype(jnp.float32)
    weighted = (lower_half + upper_half) * gates.reshape(-1)[:, None]
    moe_out = jnp.sum(weighted.reshape(local_rows, top, width), axis=1)
    mixed = (residual.astype(jnp.float32) + moe_out).astype(jnp.bfloat16)
    return (mixed, new_kv)


def solution(mesh):
    placed = (
        P(("req", "exp"), None),
        P(),
        P(None, "exp"),
        P(None, None, "exp"),
        P("req", None, "exp"),
        P("req", None, "exp"),
        P("req"),
        P("req", None),
        P("req"),
        P("req", None),
        P("exp", None),
        P(),
        P(("req", "exp"), None),
        P(("req", "exp"), None),
        P(("req", "exp"), None, None),
        P(("req", "exp"), None, None),
    )
    return jax.shard_map(
        body,
        mesh=mesh,
        in_specs=placed,
        out_specs=(P(("req", "exp"), None), P(None, "req", "exp")),
        check_vma=False,
    )
```

profile of v0, /device:TPU:11, one launch (start us, length us, event | category | flops | bytes accessed | tf_op | source)
XLA Modules:
  0.0 804.4 jit_solution(2882999910094665080)
XLA Ops:
  17.7 5.6 gather_fusion.2
  27.6 54.8 %all-gather.2.cloned.1.call-done = bf16[2048,2048]{1,0:T(8,128)(2,1)} async-done(((bf16[128,2048]{1,0:T(8,128)(2,1)}), bf16[2048,2048]{1,0:T(8,128)(2,1)}) %all-gather.2.cloned.1.call-update) | async-done | bytes 8388624 | tf_op jit(solution)/shard_map/all_gather | solution.py:94
  82.3 9.5 %fusion.100 = (bf16[2048,384]{1,0:T(8,128)(2,1)}, f32[2048,384]{1,0:T(8,128)S(1)}) fusion(bf16[2048,2048]{1,0:T(8,128)(2,1)} %all-gather.2.cloned.1.call-done, bf16[2048,128]{1,0:T(8,128)(2,1)} %get-tuple-element.261, bf16[2048,128]{1,0:T(8,128)(2,1)} %get-tuple-element.260, bf16[2048,128]{1,0:T(8,128)(2,1)} %param.20), kind=kOutput, calls=%fused_computation.173 | convolution fusion | flops 3226730496 | bytes 14680064 | tf_op jit(solution)/shard_map/dot_general | solution.py:93
  91.9 5.6 fusion.54
  98.2 7.7 fusion.13
  105.8 88.9 %while.18 = (s32[]{:T(128)}, f32[2044]{0:T(1024)S(1)}, f32[2044]{0:T(1024)S(1)}, f32[2044,128]{1,0:T(8,128)}, s32[]{:T(128)}, /*index=5*/s32[1,32]{1,0:T(1,128)S...) while((s32[]{:T(128)}, f32[2044]{0:T(1024)S(1)}, ...), condition=%wide.region_6.7_spmd.clone, body=%wide.region_3.6_spmd.clone.sunk | while | flops 548139520 | bytes 24478808 | solution.py:170
  199.5 8.4 %fusion.11 = f32[2044]{0:T(1024)S(1)} fusion(f32[2044,2044]{0,1:T(8,128)} %get-tuple-element.278, f32[2044]{0:T(1024)S(1)} %is-finite_select_fusion.1), kind=kLoop, calls=%fused_computation.32 | loop fusion | flops 20887636 | bytes 16728096 | tf_op jit(solution)/shard_map/reduce_sum | solution.py:45
  210.2 7.1 fusion.32
  217.3 5.6 convolution_convert_fusion.1
  225.0 31.1 %reduce-window.6 = s32[64,8,128]{2,1,0:T(8,128)S(1)} reduce-window(s32[64,8,128]{2,1,0:T(8,128)} %fusion.77, s32[]{:T(128)} %constant.118.clone.1), window={size=1x1x128 pad=0_0x0_0x127_0}, to_apply=%region_10.11 | reduce-window | flops 8323072 | bytes 524292 | tf_op jit(solution)/shard_map/reduce-window
  258.4 48.6 %reduce-scatter.2.cloned.1.call-done = bf16[128,2048]{1,0:T(8,128)(2,1)} async-done(((bf16[2048,2048]{1,0:T(8,128)(2,1)}), bf16[128,2048]{1,0:T(8,128)(2,1)}) %reduce-scatter.2.cloned.1.call-update) | async-done | bytes 524304 | tf_op jit(solution)/shard_map/reduce_scatter | solution.py:176
  310.4 23.5 %scatter_custom_fusion = bf16[1280,2048]{1,0:T(8,128)(2,1)} fusion(s32[1024]{0:T(1024)S(1)} %bitcast.129, bf16[128,2048]{1,0:T(8,128)(2,1)} %fusion.63, s32[1024]{0:T(1024)S(1)} %broadcast_clamp_fusion.2, bf16[]{:T(256)} %constant.122.clone.1), kind=kCustom, calls=%fused_computation.44 | custom fusion | bytes 5243392 | tf_op jit(solution)/shard_map/scatter | solution.py:196
  333.9 8.9 %broadcast_in_dim.113 = bf16[64,20,2048]{2,1,0:T(8,128)(2,1)} reshape(bf16[1280,2048]{1,0:T(8,128)(2,1)} %scatter_custom_fusion) | data formatting | bytes 10485760 | tf_op jit(solution)/shard_map/broadcast_in_dim | solution.py:198
  348.1 152.2 %all_to_all.10 = bf16[128,20,2048]{2,1,0:T(8,128)(2,1)} all-to-all(bf16[128,20,2048]{2,1,0:T(8,128)(2,1)S(1)} %bitcast.113), channel_id=1, replica_groups=mesh['req'=8,'exp'=16] {'req','exp'}, dimensions={0} | all-to-all | bytes 20971520 | tf_op jit(solution)/shard_map/all_to_all | solution.py:53
  500.2 16.5 %reshape.523 = bf16[2560,2048]{1,0:T(8,128)(2,1)} reshape(bf16[128,20,2048]{2,1,0:T(8,128)(2,1)} %all_to_all.10) | data formatting | bytes 20971520 | tf_op jit(solution)/shard_map/reshape | solution.py:204
  516.7 15.2 %fusion.18 = f32[2560,1024]{1,0:T(8,128)S(1)} fusion(bf16[2560,2048]{1,0:T(8,128)(2,1)} %reshape.523, bf16[1,2048,1024]{2,1,0:T(8,128)(2,1)} %param.32), kind=kOutput, calls=%fused_computation.42 | convolution fusion | flops 10737418240 | bytes 25165824 | tf_op jit(solution)/shard_map/dot_general | solution.py:203
  531.9 8.3 %convolution_convert_fusion = bf16[2560,2048]{1,0:T(8,128)(2,1)} fusion(f32[2560,1024]{1,0:T(8,128)S(1)} %fusion.18, bf16[1,512,2048]{2,1,0:T(8,128)(2,1)S(1)} %copy-done), kind=kOutput, calls=%fused_computation.34 | convolution fusion | flops 5381816320 | bytes 23068672 | tf_op jit(solution)/shard_map/dot_general | solution.py:208
  540.2 16.4 %reshape.524 = bf16[128,20,2048]{2,1,0:T(8,128)(2,1)} reshape(bf16[2560,2048]{1,0:T(8,128)(2,1)} %convolution_convert_fusion) | data formatting | bytes 20971520 | tf_op jit(solution)/shard_map/reshape | solution.py:210
  556.6 6.5 all-to-all-start.1
  566.7 177.0 %all-to-all-done.1 = bf16[128,20,2048]{2,1,0:T(8,128)(2,1)} async-done(((bf16[128,20,2048]{2,1,0:T(8,128)(2,1)}), bf16[128,20,2048]{2,1,0:T(8,128)(2,1)}, u32[]{:S(2)}, u32[]{:S(2)}) %all-to-all-start.1) | async-done | bytes 10485792 | tf_op jit(solution)/shard_map/all_to_all | solution.py:58
  743.7 16.5 %reshape.525 = bf16[2560,2048]{1,0:T(8,128)(2,1)} reshape(bf16[128,20,2048]{2,1,0:T(8,128)(2,1)} %all-to-all-done.1) | data formatting | bytes 20971520 | tf_op jit(solution)/shard_map/reshape | solution.py:212
  760.2 14.2 %gather_fusion.5 = bf16[1024,2048]{1,0:T(8,128)(2,1)} fusion(bf16[2560,2048]{1,0:T(8,128)(2,1)} %reshape.525, s32[1024]{0:T(1024)S(1)} %broadcast_clamp_fusion), kind=kCustom, calls=%fused_computation.6 | custom fusion | bytes 8392704 | tf_op jit(solution)/shard_map/gather | solution.py:215
  774.3 14.2 %gather_fusion.4 = bf16[1024,2048]{1,0:T(8,128)(2,1)} fusion(bf16[2560,2048]{1,0:T(8,128)(2,1)} %reshape.525, s32[1024]{0:T(1024)S(1)} %broadcast_clamp_fusion.1), kind=kCustom, calls=%fused_computation.5 | custom fusion | bytes 8392704 | tf_op jit(solution)/shard_map/gather | solution.py:214
  788.5 7.6 fusion.14
  (212 shorter events, 127.5 us)
Async XLA Ops:
  7.2 524.7 %copy-start = (bf16[1,512,2048]{2,1,0:T(8,128)(2,1)S(1)}, bf16[1,512,2048]{2,1,0:T(8,128)(2,1)}, u32[]{:S(2)}) copy-start(bf16[1,512,2048]{2,1,0:T(8,128)(2,1)} %param.33) | copy-start | bytes 6291460
  7.2 75.1 %all-gather.2.cloned.1.call-start = ((), (), s32[]{:S(2)}) async-start(), calls=%async_computation.3 | async-start | bytes 8912896 | tf_op jit(solution)/shard_map/all_gather | solution.py:94
  10.7 296.4 %reduce-scatter.2.cloned.1.call-start = ((), (), s32[]{:S(2)}) async-start(), calls=%async_computation.4 | async-start | bytes 8912896 | tf_op jit(solution)/shard_map/reduce_scatter | solution.py:176
  17.7 5.6 copy-start.10
  17.7 8.8 %copy-start.6 = (bf16[2,2048,128]{2,1,0:T(8,128)(2,1)S(1)}, bf16[2,2048,128]{2,1,0:T(8,128)(2,1)}, u32[]{:S(2)}) copy-start(bf16[2,2048,128]{2,1,0:T(8,128)(2,1)} %param.21) | copy-start | bytes 3145732
  97.5 8.3 %copy-start.4 = (bf16[2048,1,64]{2,0,1:T(8,128)(2,1)}, bf16[2048,1,64]{2,0,1:T(8,128)(2,1)S(1)}, u32[]{:S(2)}) copy-start(bf16[2048,1,64]{2,0,1:T(8,128)(2,1)S(1)} %get-tuple-element.257) | copy-start | bytes 786436
  98.2 7.7 copy-start.12
  112.7 1.7 copy-start.13
  123.8 1.7 copy-start.13
  134.9 1.7 copy-start.13
  146.1 1.7 copy-start.13
  157.2 1.7 copy-start.13
  168.3 1.7 copy-start.13
  179.4 1.7 copy-start.13
  190.5 1.7 copy-start.13
  194.8 4.0 copy-start.1
  198.8 10.6 %copy-start.15 = (f32[2044,128]{1,0:T(8,128)S(1)}, f32[2044,128]{1,0:T(8,128)}, u32[]{:S(2)}) copy-start(f32[2044,128]{1,0:T(8,128)} %get-tuple-element.158) | copy-start | bytes 3139588
  199.5 10.8 %copy-start.2 = (f32[2044,2044]{0,1:T(8,128)S(1)}, f32[2044,2044]{0,1:T(8,128)}, u32[]{:S(2)}) copy-start(f32[2044,2044]{0,1:T(8,128)} %get-tuple-element.278) | copy-start | bytes 50135236
  210.2 7.1 copy-start.7
  222.9 84.2 %copy-start.3 = (bf16[128,2048]{1,0:T(8,128)(2,1)S(1)}, bf16[128,2048]{1,0:T(8,128)(2,1)}, u32[]{:S(2)}) copy-start(bf16[128,2048]{1,0:T(8,128)(2,1)} %param.18) | copy-start | bytes 1572868
  222.9 85.5 %copy-start.11 = (f32[2048]{0:T(1024)S(1)}, f32[2048]{0:T(1024)}, u32[]{:S(2)}) copy-start(f32[2048]{0:T(1024)} %param.29) | copy-start | bytes 24580
  556.6 6.5 copy-start.8
  556.6 187.1 %all-to-all-start.1 = ((bf16[128,20,2048]{2,1,0:T(8,128)(2,1)}), bf16[128,20,2048]{2,1,0:T(8,128)(2,1)}, u32[]{:S(2)}, u32[]{:S(2)}) async-start(bf16[128,20,2048]{2,1,0:T(8,128)(2,1)} %reshape.524), calls=%async_computation.2 | async-start | bytes 25165824 | tf_op jit(solution)/shard_map/all_to_all | solution.py:58
  788.5 7.7 copy-start.5
  (9 other events, 8.5 us)
Sparse Core Ops, SparseCore 0:
  10.8 71.4 all-gather.1
  223.0 83.9 reduce-scatter.1
where the time goes:
time: 814 us; the launch traced here: 804 us
  waiting for transfers between devices  280 us (34%)
  local copies, waits for them, and re-layouts  191 us (23%)
  blocking collectives  152 us (19%)
  other arithmetic  83.1 us (10%)
  matrix products  75.5 us (9%)
  between operations  15.4 us (2%)
    all_to_all x1, waiting for transfers between devices, bring_back(): lax.all_to_all(buffer, ('req', 'exp'), split_axis=0, concat_axis=0, tiled...  177 us
    all_to_all x1, blocking collectives, deliver(): lax.all_to_all(buffer, ('req', 'exp'), split_axis=0, concat_axis=0, tiled...  152 us
    all_gather x1, waiting for transfers between devices, body(): lax.all_gather(normed_attn, 'exp', axis=0, tiled=True)  54.8 us
    reduce_scatter x1, waiting for transfers between devices, body(): lax.psum_scatter(jnp.dot(attended, w_out, preferred_element_type=jnp.floa...  48.6 us
    another operation x4, other arithmetic  36.9 us
    gather x8, local copies, waits for them, and re-layouts, prefix_step(): block_k = k_pool[chosen].reshape(block_keys, HD)  24.5 us
    gather x8, local copies, waits for them, and re-layouts, prefix_step(): block_v = v_pool[chosen].reshape(block_keys, HD)  24.5 us
    scatter x1, local copies, waits for them, and re-layouts, body(): jnp.zeros((experts * capacity, width), jnp.bfloat16).at[target]  23.5 us
  transfers between devices with their start and end apart: 3, of which 3 were waited for; matrix products, arithmetic and copies ran while one was open for 7% of the time, Pallas kernels for 0%

commit v1 on v0

v1 whole, which is shorter than its diff:
```python
import functools
import math

import jax
import jax.numpy as jnp
from jax import lax
from jax.experimental import pallas as pl
from jax.experimental.pallas import tpu as pltpu
from jax.sharding import PartitionSpec as P

HD = 128
SPLIT = 2
EPSILON = 1e-05
THETA = 10000.0
LOW = -1e30
ROWS = 256
KEYS = 1024
VMEM_LIMIT = 56 * 1024 * 1024


def rms_scale(inputs, gain):
    values = inputs.astype(jnp.float32)
    mean_square = jnp.mean(values * values, axis=-1, keepdims=True)
    return (values * lax.rsqrt(mean_square + EPSILON) * gain).astype(jnp.bfloat16)


def rotation_tables(positions):
    half = HD // 2
    steps = jnp.arange(half, dtype=jnp.float32)
    frequency = jnp.exp(steps * (-2.0 * math.log(THETA) / HD))
    angles = positions.astype(jnp.float32)[:, None] * frequency[None, :]
    cosine = jnp.cos(angles)
    sine = jnp.sin(angles)
    return (
        jnp.concatenate([cosine, cosine], axis=1),
        jnp.concatenate([-sine, sine], axis=1),
    )


def scores_of(query, keys):
    return lax.dot_general(
        query, keys, (((1,), (1,)), ((), ())), preferred_element_type=jnp.float32
    )


def fold(state, scores, values, factor):
    old_max, old_total, running = state
    new_max = jnp.maximum(old_max, jnp.max(scores, axis=1, keepdims=True))
    shrink = jnp.exp2((old_max - new_max) * factor)
    weights = jnp.exp2((scores - new_max) * factor)
    total = old_total * shrink + jnp.sum(weights, axis=1, keepdims=True)
    running = running * shrink + jnp.dot(
        weights.astype(jnp.bfloat16), values, preferred_element_type=jnp.float32
    )
    return new_max, total, running


def attention_kernel(
    dec_len_ref,
    pre_pos_ref,
    rows_ref,
    weight_ref,
    cos_ref,
    sin_ref,
    dec_k_ref,
    dec_v_ref,
    pre_k_ref,
    pre_v_ref,
    attended_ref,
    new_ref,
    own_k,
    own_v,
):
    dec_count = dec_k_ref.shape[0]
    block = pl.program_id(0)
    factor = math.log2(math.e) / math.sqrt(HD)
    mixed = jnp.dot(rows_ref[...], weight_ref[...], preferred_element_type=jnp.float32)
    cosine = cos_ref[...]
    sine = sin_ref[...]

    def rotated(values):
        return (values * cosine + pltpu.roll(values, HD // 2, 1) * sine).astype(jnp.bfloat16)

    query = rotated(mixed[:, :HD])
    keys = rotated(mixed[:, HD : 2 * HD])
    values = mixed[:, 2 * HD :].astype(jnp.bfloat16)
    new_ref[0] = keys
    new_ref[1] = values
    own_k[block] = keys
    own_v[block] = values

    row = lax.broadcasted_iota(jnp.int32, (ROWS, ROWS), 0)
    col = lax.broadcasted_iota(jnp.int32, (ROWS, ROWS), 1)
    first = jnp.where(block == 0, dec_count, 0)
    scores = jnp.where((col <= row) & (col >= first), scores_of(query, keys), LOW)
    state = fold(
        (
            jnp.full((ROWS, 1), LOW, jnp.float32),
            jnp.zeros((ROWS, 1), jnp.float32),
            jnp.zeros((ROWS, HD), jnp.float32),
        ),
        scores,
        values,
        factor,
    )

    def own_step(index, state):
        scores = jnp.where(
            col >= dec_count - index * ROWS, scores_of(query, own_k[index]), LOW
        )
        return fold(state, scores, own_v[index], factor)

    state = lax.fori_loop(0, block, own_step, state)
    length = pre_pos_ref[0]
    whole = length // KEYS

    def prefix_step(index, state):
        at = pl.ds(pl.multiple_of(index * KEYS, KEYS), KEYS)
        return fold(state, scores_of(query, pre_k_ref[at, :]), pre_v_ref[at, :], factor)

    def last_step(index, state):
        at = pl.ds(pl.multiple_of(index * KEYS, KEYS), KEYS)
        slot = lax.broadcasted_iota(jnp.int32, (ROWS, KEYS), 1) + index * KEYS
        scores = jnp.where(slot < length, scores_of(query, pre_k_ref[at, :]), LOW)
        return fold(state, scores, pre_v_ref[at, :], factor)

    state = lax.fori_loop(0, whole, prefix_step, state)
    state = lax.fori_loop(whole, pl.cdiv(length, KEYS), last_step, state)
    attended_ref[...] = (state[2] / state[1]).astype(jnp.bfloat16)

    @pl.when(block == 0)
    def _():
        head = 16
        few = query[:head]
        few_k = keys[:head].astype(jnp.float32)
        few_v = values[:head].astype(jnp.float32)
        own_scores = jnp.sum(few.astype(jnp.float32) * few_k, axis=1, keepdims=True)
        result = attended_ref[0:head, :].astype(jnp.float32)
        at_row = lax.broadcasted_iota(jnp.int32, (head, HD), 0)
        cache = dec_k_ref.shape[1]
        slot = lax.broadcasted_iota(jnp.int32, (head, cache), 1)
        for request in range(dec_count):
            scores = jnp.where(
                slot < dec_len_ref[request], scores_of(few, dec_k_ref[request]), LOW
            )
            highest = jnp.maximum(jnp.max(scores, axis=1, keepdims=True), own_scores)
            weights = jnp.exp2((scores - highest) * factor)
            own_weight = jnp.exp2((own_scores - highest) * factor)
            total = jnp.sum(weights, axis=1, keepdims=True) + own_weight
            summed = jnp.dot(
                weights.astype(jnp.bfloat16),
                dec_v_ref[request],
                preferred_element_type=jnp.float32,
            )
            summed = summed + own_weight.astype(jnp.bfloat16).astype(jnp.float32) * few_v
            result = jnp.where(at_row == request, summed / total, result)
        attended_ref[0:head, :] = result.astype(jnp.bfloat16)


def attention(rows, weight, cosine, sine, dec_k, dec_v, pre_k, pre_v, dec_len, pre_pos):
    count, width = rows.shape
    blocks = count // ROWS
    whole = lambda: pl.BlockSpec(memory_space=pltpu.VMEM)
    spec = pltpu.PrefetchScalarGridSpec(
        num_scalar_prefetch=2,
        grid=(blocks,),
        in_specs=[
            pl.BlockSpec((ROWS, width), lambda i, *_: (i, 0)),
            whole(),
            pl.BlockSpec((ROWS, HD), lambda i, *_: (i, 0)),
            pl.BlockSpec((ROWS, HD), lambda i, *_: (i, 0)),
            whole(),
            whole(),
            whole(),
            whole(),
        ],
        out_specs=[
            pl.BlockSpec((ROWS, HD), lambda i, *_: (i, 0)),
            pl.BlockSpec((2, ROWS, HD), lambda i, *_: (0, i, 0)),
        ],
        scratch_shapes=[
            pltpu.VMEM((blocks, ROWS, HD), jnp.bfloat16),
            pltpu.VMEM((blocks, ROWS, HD), jnp.bfloat16),
        ],
    )
    return pl.pallas_call(
        attention_kernel,
        grid_spec=spec,
        out_shape=[
            jax.ShapeDtypeStruct((count, HD), jnp.bfloat16),
            jax.ShapeDtypeStruct((2, count, HD), jnp.bfloat16),
        ],
        compiler_params=pltpu.CompilerParams(
            dimension_semantics=("arbitrary",), vmem_limit_bytes=VMEM_LIMIT
        ),
        cost_estimate=pl.CostEstimate(
            flops=2 * count * width * 3 * HD + 4 * count * 5120 * HD,
            bytes_accessed=24 * 1024 * 1024,
            transcendentals=count * 5120,
        ),
        name="attend",
    )(dec_len, pre_pos, rows, weight, cosine, sine, dec_k, dec_v, pre_k, pre_v)


def body(
    hidden,
    attn_gain,
    w_query,
    w_keyval,
    k_pool,
    v_pool,
    dec_len,
    dec_pages,
    pre_pos,
    pre_pages,
    w_out,
    moe_gain,
    expert_ids,
    router_logits,
    w_in,
    w_down,
):
    local_rows, width = hidden.shape
    req_count = lax.axis_size("req")
    exp_count = lax.axis_size("exp")
    devices = req_count * exp_count
    group_rows = local_rows * exp_count
    dec_count = dec_len.shape[0]
    page_size = k_pool.shape[1]
    normed_attn = rms_scale(hidden, attn_gain)
    joined = jnp.concatenate([w_query, w_keyval[0], w_keyval[1]], axis=1)
    row_index = jnp.arange(group_rows, dtype=jnp.int32)
    positions = pre_pos[0] + row_index - dec_count
    for request in range(dec_count):
        positions = jnp.where(row_index == request, dec_len[request], positions)
    cosine, sine = rotation_tables(positions)
    cache_len = dec_pages.shape[1] * page_size
    dec_k = k_pool[dec_pages].reshape(dec_count, cache_len, HD)
    dec_v = v_pool[dec_pages].reshape(dec_count, cache_len, HD)
    pre_k = k_pool[pre_pages[0]].reshape(-1, HD)
    pre_v = v_pool[pre_pages[0]].reshape(-1, HD)

    experts = devices // SPLIT
    top = expert_ids.shape[1]
    capacity = 2 * ((local_rows * top * 5 + 8 * experts - 1) // (8 * experts))
    gates = jax.nn.softmax(router_logits, axis=-1)
    expert_index = jnp.arange(experts, dtype=jnp.int32)
    chosen = expert_ids[:, :, None] == expert_index[None, None, :]
    named = jnp.sum(chosen.astype(jnp.float32), axis=1)
    gate_of = jnp.sum(jnp.where(chosen, gates[:, :, None], 0.0), axis=1)
    token = jnp.arange(local_rows, dtype=jnp.int32)
    earlier = (token[None, :] < token[:, None]).astype(jnp.bfloat16)
    place = jnp.dot(earlier, named.astype(jnp.bfloat16), preferred_element_type=jnp.float32)
    place = jnp.where(named > 0, place, -1.0)
    slot = jnp.arange(capacity, dtype=jnp.int32).astype(jnp.float32)
    taken = place.T[:, None, :] == slot[None, :, None]
    pick = taken.astype(jnp.bfloat16).reshape(experts * capacity, local_rows)
    merge = jnp.where(place[:, :, None] == slot[None, None, :], gate_of[:, :, None], 0.0)

    rows, cosine, sine, dec_k, dec_v, pre_k, pre_v, joined = lax.optimization_barrier(
        (
            lax.all_gather(normed_attn, "exp", axis=0, tiled=True),
            cosine,
            sine,
            dec_k,
            dec_v,
            pre_k,
            pre_v,
            joined,
        )
    )
    later_w_out, rows = lax.optimization_barrier((w_out, rows))
    full_w_out = lax.all_gather(later_w_out, "exp", axis=0, tiled=True)
    attended, new_kv = attention(
        rows, joined, cosine, sine, dec_k, dec_v, pre_k, pre_v, dec_len, pre_pos
    )
    by_head = lax.all_to_all(
        attended.reshape(exp_count, local_rows, HD), "exp", split_axis=0, concat_axis=0, tiled=True
    )
    own_heads = jnp.swapaxes(by_head, 0, 1).reshape(local_rows, exp_count * HD)
    projected = jnp.dot(own_heads, full_w_out, preferred_element_type=jnp.float32)
    residual = (hidden.astype(jnp.float32) + projected).astype(jnp.bfloat16)
    normed_moe = rms_scale(residual, moe_gain)

    outgoing = jnp.dot(pick, normed_moe, preferred_element_type=jnp.float32).astype(jnp.bfloat16)
    doubled = jnp.broadcast_to(
        outgoing.reshape(experts, 1, capacity, width), (experts, SPLIT, capacity, width)
    ).reshape(devices, capacity, width)
    arrived = lax.all_to_all(doubled, ("req", "exp"), split_axis=0, concat_axis=0, tiled=True)
    piece_units = w_down.shape[1]
    inner = jnp.dot(
        arrived.reshape(devices * capacity, width), w_in[0], preferred_element_type=jnp.float32
    )
    activated = (jax.nn.silu(inner[:, :piece_units]) * inner[:, piece_units:]).astype(jnp.bfloat16)
    partial_value = (
        jnp.dot(activated, w_down[0], preferred_element_type=jnp.float32)
        .astype(jnp.bfloat16)
        .reshape(devices, capacity, width)
    )
    returned = lax.all_to_all(
        partial_value, ("req", "exp"), split_axis=0, concat_axis=0, tiled=True
    ).reshape(devices * capacity, width)
    coarse = merge.astype(jnp.bfloat16)
    fine = (merge - coarse.astype(jnp.float32)).astype(jnp.bfloat16)
    weights = jnp.concatenate([coarse, fine], axis=0).reshape(2 * local_rows, experts, 1, capacity)
    weights = jnp.broadcast_to(
        weights, (2 * local_rows, experts, SPLIT, capacity)
    ).reshape(2 * local_rows, devices * capacity)
    summed = jnp.dot(weights, returned, preferred_element_type=jnp.float32)
    moe_out = summed[:local_rows] + summed[local_rows:]
    mixed = (residual.astype(jnp.float32) + moe_out).astype(jnp.bfloat16)
    return (mixed, new_kv)


def solution(mesh):
    placed = (
        P(("req", "exp"), None),
        P(),
        P(None, "exp"),
        P(None, None, "exp"),
        P("req", None, "exp"),
        P("req", None, "exp"),
        P("req"),
        P("req", None),
        P("req"),
        P("req", None),
        P("exp", None),
        P(),
        P(("req", "exp"), None),
        P(("req", "exp"), None),
        P(("req", "exp"), None, None),
        P(("req", "exp"), None, None),
    )
    return jax.shard_map(
        body,
        mesh=mesh,
        in_specs=placed,
        out_specs=(P(("req", "exp"), None), P(None, "req", "exp")),
        check_vma=False,
    )
```

time: 814 us -> 612 us (0.75)
  local copies, waits for them, and re-layouts: 191 us -> 91.9 us
  other arithmetic: 83.1 us -> 16.5 us
  Pallas kernels: 0 us -> 49.1 us
  waiting for transfers between devices: 280 us -> 235 us
  matrix products: 75.5 us -> 38.6 us
    gather x21 -> x4, local copies, waits for them, and re-layouts: 89 us -> 19.9 us  [the longest x1 5.64 us: body(): dec_v = v_pool[dec_pages].reshape(dec_count, cache_len, HD)]
    pallas_call x0 -> x1, Pallas kernels: none -> 49.1 us  [attention(): pl.pallas_call(attention_kernel, grid_spec=spec, out_shape=[jax.ShapeDtyp...]
    reduce_scatter x1 -> x0, waiting for transfers between devices: 48.6 us -> none  [body(): lax.psum_scatter(jnp.dot(attended, w_out, preferred_element_type=jnp.floa...]
    another operation x5 -> x0, other arithmetic: 39.2 us -> none
    dot_general x22 -> x4, matrix products: 52 us -> 15.1 us  [the longest x1 6 us: body(): summed = jnp.dot(weights, returned, preferred_element_type=jnp.float32)]
    reduce_sum x12 -> x1, other arithmetic: 23.8 us -> 0.05 us  [body(): named = jnp.sum(chosen.astype(jnp.float32), axis=1)]
    scatter x1 -> x0, local copies, waits for them, and re-layouts: 23.5 us -> none  [body(): jnp.zeros((experts * capacity, width), jnp.bfloat16).at[target]]
    all_gather x1, waiting for transfers between devices: 54.8 us -> 38.7 us  [body(): lax.all_gather(normed_attn, 'exp', axis=0, tiled=True)]
  transfers between devices with their start and end apart: 3 -> 4, of which waited for: 3 -> 4; matrix products, arithmetic and copies ran while one was open for 7% -> 7% of each run, Pallas kernels for 0% -> 8%
where the time goes in v1:
time: 612 us; the launch traced here: 609 us
  waiting for transfers between devices  235 us (38%)
  blocking collectives  151 us (25%)
  local copies, waits for them, and re-layouts  91.9 us (15%)
  Pallas kernels  49.1 us (8%)
  matrix products  38.6 us (6%)
  other arithmetic  16.5 us (3%)
  between operations  14.9 us (2%)
  starting transfers between devices  12.6 us (2%)
    all_to_all x1, waiting for transfers between devices, body(): lax.all_to_all(partial_value, ('req', 'exp'), split_axis=0, concat_axis=0...  177 us
    all_to_all x1, blocking collectives, body(): lax.all_to_all(doubled, ('req', 'exp'), split_axis=0, concat_axis=0, tile...  151 us
    pallas_call x1, Pallas kernels, attention(): pl.pallas_call(attention_kernel, grid_spec=spec, out_shape=[jax.ShapeDtyp...  49.1 us
    all_gather x1, waiting for transfers between devices, body(): lax.all_gather(normed_attn, 'exp', axis=0, tiled=True)  38.7 us
    reshape x1, local copies, waits for them, and re-layouts, body(): arrived.reshape(devices * capacity, width)  16.5 us
    reshape x1, local copies, waits for them, and re-layouts, body(): returned = lax.all_to_all(partial_value, ('req', 'exp'), split_axis=0, co...  16.5 us
    reshape x1, local copies, waits for them, and re-layouts, body(): partial_value = jnp.dot(activated, w_down[0], preferred_element_type=jnp....  16.4 us
    dot_general x1, matrix products, body(): jnp.dot(arrived.reshape(devices * capacity, width), w_in[0], preferred_el...  15.2 us
  transfers between devices with their start and end apart: 4, of which 4 were waited for; matrix products, arithmetic and copies ran while one was open for 7% of the time, Pallas kernels for 8%

profile of v1, /device:TPU:11, one launch (start us, length us, event | category | flops | bytes accessed | tf_op | source)
XLA Modules:
  0.0 609.0 jit_solution(7779990896361918522)
XLA Ops:
  11.5 5.5 gather_fusion
  17.0 5.6 gather_fusion.1
  22.7 4.5 gather_fusion.3
  27.2 4.3 gather_fusion.2
  38.0 3.7 fusion.17
  43.7 38.7 %all-gather.3.cloned.1.call-done.rows_ref = bf16[2048,2048]{1,0:T(8,128)(2,1)} async-done(((bf16[128,2048]{1,0:T(8,128)(2,1)}), bf16[2048,2048]{1,0:T(8,128)(2,1)}) %all-gather.3.cloned.1.call-update) | async-done | bytes 8388624 | tf_op jit(solution)/shard_map/all_gather | solution.py:262
  82.4 49.1 %attend.1 = (bf16[2048,128]{1,0:T(8,128)(2,1)}, bf16[2,2048,128]{2,1,0:T(8,128)(2,1)}) custom-call(s32[4]{0:T(128)} %dec_len_ref.1, s32[1]{0:T(128)} %copy.25.pre_pos_ref, bf16[2048,2048]{1,0:T(8,128)(2,1)} %all-gather.3.cloned.1.call-done.rows_ref, bf16[2048,384]{1,0:T(8,128)(2,1)} %pad_maximum_fusion.weight_ref, f32[2048,128]{1,0:T(8,128)} %get-tuple-element.17.cos_ref, ...), custom_call_target="tpu_custom_call" | custom-call | flops 8589934592 | bytes 25165824 | tf_op jit(solution)/shard_map/attend/pallas_call | solution.py:186
  133.5 6.4 %all-to-all-start = ((bf16[16,128,128]{1,2,0:T(8,128)(2,1)}), bf16[16,128,128]{1,2,0:T(8,128)(2,1)S(1)}, u32[]{:S(2)}, u32[]{:S(2)}) async-start(bf16[16,128,128]{1,2,0:T(8,128)(2,1)} %copy.24), calls=%async_computation | async-start | bytes 1048576 | tf_op jit(solution)/shard_map/all_to_all | solution.py:277
  141.2 11.0 %all-to-all-done = bf16[16,128,128]{1,2,0:T(8,128)(2,1)S(1)} async-done(((bf16[16,128,128]{1,2,0:T(8,128)(2,1)}), bf16[16,128,128]{1,2,0:T(8,128)(2,1)S(1)}, u32[]{:S(2)}, u32[]{:S(2)}) %all-to-all-start) | async-done | bytes 524320 | tf_op jit(solution)/shard_map/all_to_all | solution.py:277
  152.2 8.3 %all-gather.5.cloned.1.call-done = bf16[2048,2048]{1,0:T(8,128)(2,1)} async-done(((bf16[128,2048]{1,0:T(8,128)(2,1)}), bf16[2048,2048]{1,0:T(8,128)(2,1)}) %all-gather.5.cloned.1.call-update) | async-done | bytes 8388624 | tf_op jit(solution)/shard_map/all_gather | solution.py:273
  160.6 5.0 multiply_reduce_fusion
  165.6 4.0 convolution_convert_fusion.1
  169.6 8.9 %broadcast_in_dim.88 = bf16[64,20,2048]{2,1,0:T(8,128)(2,1)} reshape(bf16[1280,2048]{1,0:T(8,128)(2,1)} %convolution_convert_fusion.1) | data formatting | bytes 10485760 | tf_op jit(solution)/shard_map/broadcast_in_dim | solution.py:286
  178.5 5.2 broadcast_in_dim.89
  183.8 150.7 %all_to_all.15 = bf16[128,20,2048]{2,1,0:T(8,128)(2,1)} all-to-all(bf16[128,20,2048]{2,1,0:T(8,128)(2,1)S(1)} %bitcast.37), channel_id=1, replica_groups=mesh['req'=8,'exp'=16] {'req','exp'}, dimensions={0} | all-to-all | bytes 20971520 | tf_op jit(solution)/shard_map/all_to_all | solution.py:289
  334.4 16.5 %reshape.136 = bf16[2560,2048]{1,0:T(8,128)(2,1)} reshape(bf16[128,20,2048]{2,1,0:T(8,128)(2,1)} %all_to_all.15) | data formatting | bytes 20971520 | tf_op jit(solution)/shard_map/reshape | solution.py:292
  350.9 15.2 %fusion.1 = f32[2560,1024]{1,0:T(8,128)S(1)} fusion(bf16[2560,2048]{1,0:T(8,128)(2,1)} %reshape.136, bf16[1,2048,1024]{2,1,0:T(8,128)(2,1)} %param.30), kind=kOutput, calls=%fused_computation.8 | convolution fusion | flops 10737418240 | bytes 25165824 | tf_op jit(solution)/shard_map/dot_general | solution.py:291
  366.1 8.3 %convolution_convert_fusion = bf16[2560,2048]{1,0:T(8,128)(2,1)} fusion(f32[2560,1024]{1,0:T(8,128)S(1)} %fusion.1, bf16[1,512,2048]{2,1,0:T(8,128)(2,1)S(1)} %copy-done), kind=kOutput, calls=%fused_computation.4 | convolution fusion | flops 5381816320 | bytes 23068672 | tf_op jit(solution)/shard_map/dot_general | solution.py:296
  374.4 16.4 %reshape.137 = bf16[128,20,2048]{2,1,0:T(8,128)(2,1)} reshape(bf16[2560,2048]{1,0:T(8,128)(2,1)} %convolution_convert_fusion) | data formatting | bytes 20971520 | tf_op jit(solution)/shard_map/reshape | solution.py:298
  390.8 6.1 %all-to-all-start.2 = ((bf16[128,20,2048]{2,1,0:T(8,128)(2,1)}), bf16[128,20,2048]{2,1,0:T(8,128)(2,1)}, u32[]{:S(2)}, u32[]{:S(2)}) async-start(bf16[128,20,2048]{2,1,0:T(8,128)(2,1)} %reshape.137), calls=%async_computation.2 | async-start | bytes 25165824 | tf_op jit(solution)/shard_map/all_to_all | solution.py:300
  398.7 3.3 reshape.134
  402.0 176.8 %all-to-all-done.2 = bf16[128,20,2048]{2,1,0:T(8,128)(2,1)} async-done(((bf16[128,20,2048]{2,1,0:T(8,128)(2,1)}), bf16[128,20,2048]{2,1,0:T(8,128)(2,1)}, u32[]{:S(2)}, u32[]{:S(2)}) %all-to-all-start.2) | async-done | bytes 10485792 | tf_op jit(solution)/shard_map/all_to_all | solution.py:300
  578.8 16.5 %reshape.138 = bf16[2560,2048]{1,0:T(8,128)(2,1)} reshape(bf16[128,20,2048]{2,1,0:T(8,128)(2,1)} %all-to-all-done.2) | data formatting | bytes 20971520 | tf_op jit(solution)/shard_map/reshape | solution.py:302
  595.2 6.0 fusion.25
  (53 shorter events, 18.3 us)
Async XLA Ops:
  7.2 358.9 %copy-start = (bf16[1,512,2048]{2,1,0:T(8,128)(2,1)S(1)}, bf16[1,512,2048]{2,1,0:T(8,128)(2,1)}, u32[]{:S(2)}) copy-start(bf16[1,512,2048]{2,1,0:T(8,128)(2,1)} %param.31) | copy-start | bytes 6291460
  7.2 75.1 %all-gather.3.cloned.1.call-start = ((), (), s32[]{:S(2)}) async-start(), calls=%async_computation.3 | async-start | bytes 8912896 | tf_op jit(solution)/shard_map/all_gather | solution.py:262
  10.7 149.9 %all-gather.5.cloned.1.call-start = ((), (), s32[]{:S(2)}) async-start(), calls=%async_computation.4 | async-start | bytes 8912896 | tf_op jit(solution)/shard_map/all_gather | solution.py:273
  17.0 5.6 copy-start.8
  17.0 15.1 %copy-start.5 = (s32[4]{0:T(128)S(1)}, s32[4]{0:T(128)}, u32[]{:S(2)}) copy-start(s32[4]{0:T(128)} %dec_len_ref.1) | copy-start | bytes 52
  17.0 18.4 %copy-start.3 = (bf16[2,2048,128]{2,1,0:T(8,128)(2,1)S(1)}, bf16[2,2048,128]{2,1,0:T(8,128)(2,1)}, u32[]{:S(2)}) copy-start(bf16[2,2048,128]{2,1,0:T(8,128)(2,1)} %param.19) | copy-start | bytes 3145732
  37.9 44.4 %copy-start.4 = (f32[128,8]{0,1:T(8,128)S(1)}, f32[128,8]{0,1:T(8,128)}, u32[]{:S(2)}) copy-start(f32[128,8]{0,1:T(8,128)} %param.29) | copy-start | bytes 12292
  82.4 57.6 %copy-start.7 = (s32[128,8]{0,1:T(8,128)S(1)}, s32[128,8]{0,1:T(8,128)}, u32[]{:S(2)}) copy-start(s32[128,8]{0,1:T(8,128)} %param.28) | copy-start | bytes 12292
  133.5 18.7 %all-to-all-start = ((bf16[16,128,128]{1,2,0:T(8,128)(2,1)}), bf16[16,128,128]{1,2,0:T(8,128)(2,1)S(1)}, u32[]{:S(2)}, u32[]{:S(2)}) async-start(bf16[16,128,128]{1,2,0:T(8,128)(2,1)} %copy.24), calls=%async_computation | async-start | bytes 1048576 | tf_op jit(solution)/shard_map/all_to_all | solution.py:277
  152.2 8.3 %copy-start.2 = (bf16[16,128,128]{1,2,0:T(8,128)(2,1)}, bf16[16,128,128]{1,2,0:T(8,128)(2,1)S(1)}, u32[]{:S(2)}) copy-start(bf16[16,128,128]{1,2,0:T(8,128)(2,1)S(1)} %all-to-all-done) | copy-start | bytes 1572868
  160.6 5.0 copy-start.1
  160.6 5.0 copy-start.6
  390.8 188.0 %all-to-all-start.2 = ((bf16[128,20,2048]{2,1,0:T(8,128)(2,1)}), bf16[128,20,2048]{2,1,0:T(8,128)(2,1)}, u32[]{:S(2)}, u32[]{:S(2)}) async-start(bf16[128,20,2048]{2,1,0:T(8,128)(2,1)} %reshape.137), calls=%async_computation.2 | async-start | bytes 25165824 | tf_op jit(solution)/shard_map/all_to_all | solution.py:300
Sparse Core Ops, SparseCore 0:
  10.8 71.4 all-gather.2
  84.5 76.0 all-gather.4

commit v2 on v1

--- a/solution.py
+++ b/solution.py
@@ -14,6 +14,8 @@
 THETA = 10000.0
 LOW = -1e30
 ROWS = 256
+CHAINS = 2
+STEP_ROWS = ROWS * CHAINS
 KEYS = 1024
 VMEM_LIMIT = 56 * 1024 * 1024
 
@@ -88,45 +90,59 @@
     new_ref[1] = values
     own_k[block] = keys
     own_v[block] = values
-
-    row = lax.broadcasted_iota(jnp.int32, (ROWS, ROWS), 0)
-    col = lax.broadcasted_iota(jnp.int32, (ROWS, ROWS), 1)
+    chains = [query[i * ROWS : (i + 1) * ROWS] for i in range(CHAINS)]
     first = jnp.where(block == 0, dec_count, 0)
-    scores = jnp.where((col <= row) & (col >= first), scores_of(query, keys), LOW)
-    state = fold(
-        (
+    states = []
+    for i, part in enumerate(chains):
+        span = (i + 1) * ROWS
+        row = lax.broadcasted_iota(jnp.int32, (ROWS, span), 0) + i * ROWS
+        col = lax.broadcasted_iota(jnp.int32, (ROWS, span), 1)
+        scores = jnp.where((col <= row) & (col >= first), scores_of(part, keys[:span]), LOW)
+        start = (
             jnp.full((ROWS, 1), LOW, jnp.float32),
             jnp.zeros((ROWS, 1), jnp.float32),
             jnp.zeros((ROWS, HD), jnp.float32),
-        ),
-        scores,
-        values,
-        factor,
-    )
-
-    def own_step(index, state):
-        scores = jnp.where(
-            col >= dec_count - index * ROWS, scores_of(query, own_k[index]), LOW
         )
-        return fold(state, scores, own_v[index], factor)
-
-    state = lax.fori_loop(0, block, own_step, state)
+        states.append(fold(start, scores, values[:span], factor))
+
+    def own_step(index, states):
+        col = lax.broadcasted_iota(jnp.int32, (1, STEP_ROWS), 1)
+        bias = jnp.where(col >= dec_count - index * STEP_ROWS, 0.0, LOW)
+        held_k = own_k[index]
+        held_v = own_v[index]
+        return [
+            fold(state, scores_of(part, held_k) + bias, held_v, factor)
+            for part, state in zip(chains, states)
+        ]
+
+    states = lax.fori_loop(0, block, own_step, states)
     length = pre_pos_ref[0]
     whole = length // KEYS
 
-    def prefix_step(index, state):
+    def prefix_step(index, states):
         at = pl.ds(pl.multiple_of(index * KEYS, KEYS), KEYS)
-        return fold(state, scores_of(query, pre_k_ref[at, :]), pre_v_ref[at, :], factor)
-
-    def last_step(index, state):
+        held_k = pre_k_ref[at, :]
+        held_v = pre_v_ref[at, :]
+        return [
+            fold(state, scores_of(part, held_k), held_v, factor)
+            for part, state in zip(chains, states)
+        ]
+
+    def last_step(index, states):
         at = pl.ds(pl.multiple_of(index * KEYS, KEYS), KEYS)
-        slot = lax.broadcasted_iota(jnp.int32, (ROWS, KEYS), 1) + index * KEYS
-        scores = jnp.where(slot < length, scores_of(query, pre_k_ref[at, :]), LOW)
-        return fold(state, scores, pre_v_ref[at, :], factor)
-
-    state = lax.fori_loop(0, whole, prefix_step, state)
-    state = lax.fori_loop(whole, pl.cdiv(length, KEYS), last_step, state)
-    attended_ref[...] = (state[2] / state[1]).astype(jnp.bfloat16)
+        slot = lax.broadcasted_iota(jnp.int32, (1, KEYS), 1) + index * KEYS
+        bias = jnp.where(slot < length, 0.0, LOW)
+        held_k = pre_k_ref[at, :]
+        held_v = pre_v_ref[at, :]
+        return [
+            fold(state, scores_of(part, held_k) + bias, held_v, factor)
+            for part, state in zip(chains, states)
+        ]
+
+    states = lax.fori_loop(0, whole, prefix_step, states)
+    states = lax.fori_loop(whole, pl.cdiv(length, KEYS), last_step, states)
+    for i, state in enumerate(states):
+        attended_ref[i * ROWS : (i + 1) * ROWS, :] = (state[2] / state[1]).astype(jnp.bfloat16)
 
     @pl.when(block == 0)
     def _():
@@ -159,28 +175,28 @@
 
 def attention(rows, weight, cosine, sine, dec_k, dec_v, pre_k, pre_v, dec_len, pre_pos):
     count, width = rows.shape
-    blocks = count // ROWS
+    blocks = count // STEP_ROWS
     whole = lambda: pl.BlockSpec(memory_space=pltpu.VMEM)
     spec = pltpu.PrefetchScalarGridSpec(
         num_scalar_prefetch=2,
         grid=(blocks,),
         in_specs=[
-            pl.BlockSpec((ROWS, width), lambda i, *_: (i, 0)),
+            pl.BlockSpec((STEP_ROWS, width), lambda i, *_: (i, 0)),
             whole(),
-            pl.BlockSpec((ROWS, HD), lambda i, *_: (i, 0)),
-            pl.BlockSpec((ROWS, HD), lambda i, *_: (i, 0)),
+            pl.BlockSpec((STEP_ROWS, HD), lambda i, *_: (i, 0)),
+            pl.BlockSpec((STEP_ROWS, HD), lambda i, *_: (i, 0)),
             whole(),
             whole(),
             whole(),
             whole(),
         ],
         out_specs=[
-            pl.BlockSpec((ROWS, HD), lambda i, *_: (i, 0)),
-            pl.BlockSpec((2, ROWS, HD), lambda i, *_: (0, i, 0)),
+            pl.BlockSpec((STEP_ROWS, HD), lambda i, *_: (i, 0)),
+            pl.BlockSpec((2, STEP_ROWS, HD), lambda i, *_: (0, i, 0)),
         ],
         scratch_shapes=[
-            pltpu.VMEM((blocks, ROWS, HD), jnp.bfloat16),
-            pltpu.VMEM((blocks, ROWS, HD), jnp.bfloat16),
+            pltpu.VMEM((blocks, STEP_ROWS, HD), jnp.bfloat16),
+            pltpu.VMEM((blocks, STEP_ROWS, HD), jnp.bfloat16),
         ],
     )
     return pl.pallas_call(
@@ -200,6 +216,117 @@
         ),
         name="attend",
     )(dec_len, pre_pos, rows, weight, cosine, sine, dec_k, dec_v, pre_k, pre_v)
+
+
+PLANE_STEPS = (
+    (2, 1), (1, 2), (2, 3), (3, 2), (2, 0), (0, 2), (1, 1), (3, 3),
+    (1, 3), (3, 1), (2, 2), (1, 0), (3, 0), (0, 1), (0, 3), (0, 0),
+)
+STEPS = [(dz, dy, (i + turn) % 2) for turn in (1, 0) for i, (dz, dy) in enumerate(PLANE_STEPS)]
+STEPS.remove((0, 0, 0))
+GROUP_STEPS = PLANE_STEPS[:-1]
+SIDE = 4
+
+
+def expert_peer(step):
+    dz, dy, dx = step
+    req = lax.axis_index("req")
+    exp = lax.axis_index("exp")
+    z, core, y, x = req // 2, req % 2, exp // SIDE, exp % SIDE
+    inner = ((x + 1) // 2) % 2
+    pz, py, at = (z + dz) % SIDE, (y + dy) % SIDE, (x // 2 + dx) % 2
+    px = inner * (1 + at) + (1 - inner) * 3 * at
+    return (pz * SIDE + py) * 2 + at, (pz * 2 + core, py * SIDE + px)
+
+
+def group_peer(step):
+    dy, dx = step
+    exp = lax.axis_index("exp")
+    place = (exp // SIDE + dy) % SIDE * SIDE + (exp % SIDE + dx) % SIDE
+    return place, (lax.axis_index("req"), place)
+
+
+def exchange_kernel(peer, steps, blocks_ref, out_ref, send_sem, recv_sem, local_sem):
+    me, _ = peer((0,) * len(steps[0]))
+    barrier = pltpu.get_barrier_semaphore()
+    for step in steps:
+        pl.semaphore_signal(
+            barrier, inc=1, device_id=peer(step)[1], device_id_type=pl.DeviceIdType.MESH
+        )
+    own = pltpu.make_async_copy(blocks_ref.at[me], out_ref.at[me], local_sem)
+    own.start()
+    pl.semaphore_wait(barrier, len(steps))
+    copies = []
+    for index, step in enumerate(steps):
+        place, device = peer(step)
+        copy = pltpu.make_async_remote_copy(
+            src_ref=blocks_ref.at[place],
+            dst_ref=out_ref.at[me],
+            send_sem=send_sem.at[index],
+            recv_sem=recv_sem.at[index],
+            device_id=device,
+            device_id_type=pl.DeviceIdType.MESH,
+        )
+        copy.start()
+        copies.append(copy)
+    own.wait()
+    for copy in copies:
+        copy.wait()
+
+
+def exchange(blocks, peer, steps, number):
+    return pl.pallas_call(
+        functools.partial(exchange_kernel, peer, steps),
+        in_specs=[pl.BlockSpec(memory_space=pl.ANY)],
+        out_specs=pl.BlockSpec(memory_space=pl.ANY),
+        out_shape=jax.ShapeDtypeStruct(blocks.shape, blocks.dtype),
+        scratch_shapes=[
+            pltpu.SemaphoreType.DMA((len(steps),)),
+            pltpu.SemaphoreType.DMA((len(steps),)),
+            pltpu.SemaphoreType.DMA,
+        ],
+        compiler_params=pltpu.CompilerParams(collective_id=number, has_side_effects=True),
+        name="exchange",
+    )(blocks)
+
+
+def expert_kernel(rows_ref, in_a_ref, in_b0_ref, in_b1_ref, down_a_ref, down_b_ref, out_ref):
+    rows = rows_ref[...]
+    depth = in_b0_ref.shape[0]
+    units = down_a_ref.shape[0]
+
+    def activate(inner):
+        return (jax.nn.silu(inner[:, :units]) * inner[:, units:]).astype(jnp.bfloat16)
+
+    inner_a = jnp.dot(rows, in_a_ref[...], preferred_element_type=jnp.float32)
+    inner_b = jnp.dot(
+        rows[:, :depth], in_b0_ref[...], preferred_element_type=jnp.float32
+    ) + jnp.dot(rows[:, depth:], in_b1_ref[...], preferred_element_type=jnp.float32)
+    total = jnp.dot(
+        activate(inner_a), down_a_ref[...], preferred_element_type=jnp.float32
+    ) + jnp.dot(activate(inner_b), down_b_ref[...], preferred_element_type=jnp.float32)
+    out_ref[...] = total.astype(jnp.bfloat16)
+
+
+def expert_rows(rows, *pieces):
+    count, width = rows.shape
+    whole = lambda: pl.BlockSpec(memory_space=pltpu.VMEM)
+    return pl.pallas_call(
+        expert_kernel,
+        grid=(count // ROWS,),
+        in_specs=[pl.BlockSpec((ROWS, width), lambda i: (i, 0))] + [whole() for _ in pieces],
+        out_specs=pl.BlockSpec((ROWS, width), lambda i: (i, 0)),
+        out_shape=jax.ShapeDtypeStruct((count, width), jnp.bfloat16),
+        compiler_params=pltpu.CompilerParams(
+            dimension_semantics=("arbitrary",), vmem_limit_bytes=VMEM_LIMIT
+        ),
+        cost_estimate=pl.CostEstimate(
+            flops=2 * count * width * 3072,
+            bytes_accessed=24 * 1024 * 1024,
+            transcendentals=count * 1024,
+        ),
+        name="experts",
+    )(rows, *pieces)
 
 
 def body(
@@ -240,24 +367,42 @@
     pre_k = k_pool[pre_pages[0]].reshape(-1, HD)
     pre_v = v_pool[pre_pages[0]].reshape(-1, HD)
 
+    core = lax.axis_index("req") % 2
+    mates = [(i, i + 1 - 2 * (i % 2)) for i in range(req_count)]
+    halves = [(i, i + 1 - 2 * (i % 2)) for i in range(exp_count)]
     experts = devices // SPLIT
+    peers = experts // 2
     top = expert_ids.shape[1]
     capacity = 2 * ((local_rows * top * 5 + 8 * experts - 1) // (8 * experts))
-    gates = jax.nn.softmax(router_logits, axis=-1)
-    expert_index = jnp.arange(experts, dtype=jnp.int32)
-    chosen = expert_ids[:, :, None] == expert_index[None, None, :]
+    both_ids = jnp.concatenate([expert_ids, lax.ppermute(expert_ids, "req", mates)], axis=0)
+    both_logits = jnp.concatenate(
+        [router_logits, lax.ppermute(router_logits, "req", mates)], axis=0
+    )
+    gates = jax.nn.softmax(both_logits, axis=-1)
+    plane = exp_count // SPLIT
+    peer_index = jnp.arange(peers, dtype=jnp.int32)
+    expert_index = (peer_index // plane * 2 + core) * plane + peer_index % plane
+    chosen = both_ids[:, :, None] == expert_index[None, None, :]
     named = jnp.sum(chosen.astype(jnp.float32), axis=1)
     gate_of = jnp.sum(jnp.where(chosen, gates[:, :, None], 0.0), axis=1)
-    token = jnp.arange(local_rows, dtype=jnp.int32)
-    earlier = (token[None, :] < token[:, None]).astype(jnp.bfloat16)
+    token = jnp.arange(2 * local_rows, dtype=jnp.int32)
+    same = token[None, :] // local_rows == token[:, None] // local_rows
+    earlier = ((token[None, :] < token[:, None]) & same).astype(jnp.bfloat16)
     place = jnp.dot(earlier, named.astype(jnp.bfloat16), preferred_element_type=jnp.float32)
+    place = place + jnp.where(token >= local_rows, float(capacity), 0.0)[:, None]
     place = jnp.where(named > 0, place, -1.0)
-    slot = jnp.arange(capacity, dtype=jnp.int32).astype(jnp.float32)
+    block = 2 * capacity
+    slot = jnp.arange(block, dtype=jnp.int32).astype(jnp.float32)
     taken = place.T[:, None, :] == slot[None, :, None]
-    pick = taken.astype(jnp.bfloat16).reshape(experts * capacity, local_rows)
+    pick = taken.astype(jnp.bfloat16).reshape(peers * block, 2 * local_rows)
     merge = jnp.where(place[:, :, None] == slot[None, None, :], gate_of[:, :, None], 0.0)
-
-    rows, cosine, sine, dec_k, dec_v, pre_k, pre_v, joined = lax.optimization_barrier(
+    merge = merge.reshape(2 * local_rows, peers * block)
+    coarse = merge.astype(jnp.bfloat16)
+    fine = (merge - coarse.astype(jnp.float32)).astype(jnp.bfloat16)
+    weights = jnp.concatenate([coarse, fine], axis=0)
+
+    depth = width // 4
+    rows, cosine, sine, dec_k, dec_v, pre_k, pre_v, joined, pick, weights = lax.optimization_barrier(
         (
             lax.all_gather(normed_attn, "exp", axis=0, tiled=True),
             cosine,
@@ -267,47 +412,53 @@
             pre_k,
             pre_v,
             joined,
+            pick,
+            weights,
         )
     )
-    later_w_out, rows = lax.optimization_barrier((w_out, rows))
-    full_w_out = lax.all_gather(later_w_out, "exp", axis=0, tiled=True)
+    half = HD // 2
+    own_half = lax.dynamic_slice_in_dim(w_out, core * half, half, 0)
+    later_w_out, later_in, rows = lax.optimization_barrier((own_half, w_in[0, :depth], rows))
+    near_w_out = lax.all_gather(later_w_out, "exp", axis=0, tiled=True)
+    other_in_0 = lax.ppermute(later_in, "exp", halves)
     attended, new_kv = attention(
         rows, joined, cosine, sine, dec_k, dec_v, pre_k, pre_v, dec_len, pre_pos
     )
-    by_head = lax.all_to_all(
-        attended.reshape(exp_count, local_rows, HD), "exp", split_axis=0, concat_axis=0, tiled=True
-    )
-    own_heads = jnp.swapaxes(by_head, 0, 1).reshape(local_rows, exp_count * HD)
-    projected = jnp.dot(own_heads, full_w_out, preferred_element_type=jnp.float32)
+    attended, near_w_out, other_in_0 = lax.optimization_barrier(
+        (attended, near_w_out, other_in_0)
+    )
+    far_w_out = lax.ppermute(near_w_out, "req", mates)
+    by_head = exchange(
+        attended.reshape(exp_count, local_rows, HD), group_peer, GROUP_STEPS, 2
+    )
+    later_in, later_down, by_head = lax.optimization_barrier(
+        (w_in[0, depth:], w_down[0], by_head)
+    )
+    other_in_1 = lax.ppermute(later_in, "exp", halves)
+    other_down = lax.ppermute(later_down, "exp", halves)
+    first_half = jnp.swapaxes(by_head[:, :, :half], 0, 1).reshape(local_rows, -1)
+    second_half = jnp.swapaxes(by_head[:, :, half:], 0, 1).reshape(local_rows, -1)
+    near = jnp.where(core == 0, first_half, second_half)
+    far = jnp.where(core == 0, second_half, first_half)
+    projected = jnp.dot(near, near_w_out, preferred_element_type=jnp.float32) + jnp.dot(
+        far, far_w_out, preferred_element_type=jnp.float32
+    )
     residual = (hidden.astype(jnp.float32) + projected).astype(jnp.bfloat16)
     normed_moe = rms_scale(residual, moe_gain)
 
-    outgoing = jnp.dot(pick, normed_moe, preferred_element_type=jnp.float32).astype(jnp.bfloat16)
-    doubled = jnp.broadcast_to(
-        outgoing.reshape(experts, 1, capacity, width), (experts, SPLIT, capacity, width)
-    ).reshape(devices, capacity, width)
-    arrived = lax.all_to_all(doubled, ("req", "exp"), split_axis=0, concat_axis=0, tiled=True)
-    piece_units = w_down.shape[1]
-    inner = jnp.dot(
-        arrived.reshape(devices * capacity, width), w_in[0], preferred_element_type=jnp.float32
-    )
-    activated = (jax.nn.silu(inner[:, :piece_units]) * inner[:, piece_units:]).astype(jnp.bfloat16)
-    partial_value = (
-        jnp.dot(activated, w_down[0], preferred_element_type=jnp.float32)
-        .astype(jnp.bfloat16)
-        .reshape(devices, capacity, width)
-    )
-    returned = lax.all_to_all(
-        partial_value, ("req", "exp"), split_axis=0, concat_axis=0, tiled=True
-    ).reshape(devices * capacity, width)
-    coarse = merge.astype(jnp.bfloat16)
-    fine = (merge - coarse.astype(jnp.float32)).astype(jnp.bfloat16)
-    weights = jnp.concatenate([coarse, fine], axis=0).reshape(2 * local_rows, experts, 1, capacity)
-    weights = jnp.broadcast_to(
-        weights, (2 * local_rows, experts, SPLIT, capacity)
-    ).reshape(2 * local_rows, devices * capacity)
-    summed = jnp.dot(weights, returned, preferred_element_type=jnp.float32)
-    moe_out = summed[:local_rows] + summed[local_rows:]
+    both_rows = jnp.concatenate([normed_moe, lax.ppermute(normed_moe, "req", mates)], axis=0)
+    outgoing = jnp.dot(pick, both_rows, preferred_element_type=jnp.float32).astype(jnp.bfloat16)
+    arrived = exchange(outgoing.reshape(peers, block, width), expert_peer, STEPS, 0)
+    partial_value = expert_rows(
+        arrived.reshape(peers * block, width), w_in[0], other_in_0, other_in_1, w_down[0], other_down
+    )
+    returned = exchange(partial_value.reshape(peers, block, width), expert_peer, STEPS, 1)
+    summed = jnp.dot(
+        weights, returned.reshape(peers * block, width), preferred_element_type=jnp.float32
+    )
+    summed = summed[: 2 * local_rows] + summed[2 * local_rows :]
+    theirs = lax.ppermute(summed[local_rows:].astype(jnp.bfloat16), "req", mates)
+    moe_out = summed[:local_rows] + theirs.astype(jnp.float32)
     mixed = (residual.astype(jnp.float32) + moe_out).astype(jnp.bfloat16)
     return (mixed, new_kv)
 

time: 612 us -> 381 us (0.62)
  Pallas kernels: 49.1 us -> 206 us
  waiting for transfers between devices: 235 us -> 81.7 us
  blocking collectives: 151 us -> 0 us
  local copies, waits for them, and re-layouts: 91.9 us -> 29.9 us
  matrix products: 38.6 us -> 12.9 us
    all_to_all x2 -> x0, waiting for transfers between devices: 188 us -> none  [the longest x1 177 us: body(): lax.all_to_all(partial_value, ('req', 'exp'), split_axis=0, concat_axis=0...]
    pallas_call x0 -> x4, Pallas kernels: none -> 177 us  [the longest x3 154 us: exchange(): pl.pallas_call(functools.partial(exchange_kernel, peer, steps), in_specs=...]
    all_to_all x1 -> x0, blocking collectives: 151 us -> none  [body(): lax.all_to_all(doubled, ('req', 'exp'), split_axis=0, concat_axis=0, tile...]
    reshape x5 -> x0, local copies, waits for them, and re-layouts: 54.6 us -> none  [the longest x1 16.5 us: body(): arrived.reshape(devices * capacity, width)]
    dot_general x5 -> x4, matrix products: 38.5 us -> 12.7 us  [the longest x1 4.85 us: body(): jnp.dot(weights, returned.reshape(peers * block, width), preferred_elemen...]
    ppermute x0 -> x8, waiting for transfers between devices: none -> 24.9 us  [the longest x1 21.8 us: body(): other_down = lax.ppermute(later_down, 'exp', halves)]
    pallas_call x1, Pallas kernels: 49.1 us -> 28.8 us  [attention(): pl.pallas_call(attention_kernel, grid_spec=spec, out_shape=[jax.ShapeDtyp...]
    broadcast_in_dim x3 -> x0, local copies, waits for them, and re-layouts: 15.4 us -> none  [the longest x2 14.1 us: body(): jnp.broadcast_to(outgoing.reshape(experts, 1, capacity, width), (experts,...]
  transfers between devices with their start and end apart: 4 -> 10, of which waited for: 4 -> 5; matrix products, arithmetic and copies ran while one was open for 7% -> 14% of each run, Pallas kernels for 8% -> 31%
where the time goes in v2:
time: 381 us; the launch traced here: 374 us
  Pallas kernels  206 us (54%)
  waiting for transfers between devices  81.7 us (21%)
  local copies, waits for them, and re-layouts  29.9 us (8%)
  other arithmetic  18.4 us (5%)
  between operations  15 us (4%)
  matrix products  12.9 us (3%)
  starting transfers between devices  10.3 us (3%)
    pallas_call x3, Pallas kernels, exchange(): pl.pallas_call(functools.partial(exchange_kernel, peer, steps), in_specs=...  154 us
    all_gather x1, waiting for transfers between devices, body(): lax.all_gather(normed_attn, 'exp', axis=0, tiled=True)  33 us
    pallas_call x1, Pallas kernels, attention(): pl.pallas_call(attention_kernel, grid_spec=spec, out_shape=[jax.ShapeDtyp...  28.8 us
    all_gather x1, waiting for transfers between devices, body(): near_w_out = lax.all_gather(later_w_out, 'exp', axis=0, tiled=True)  23.7 us
    pallas_call x1, Pallas kernels, expert_rows(): pl.pallas_call(expert_kernel, grid=(count // ROWS,), in_specs=[pl.BlockSp...  23.5 us
    ppermute x1, waiting for transfers between devices, body(): other_down = lax.ppermute(later_down, 'exp', halves)  21.8 us
  transfers between devices with their start and end apart: 10, of which 5 were waited for; matrix products, arithmetic and copies ran while one was open for 14% of the time, Pallas kernels for 31%

profile of v2, /device:TPU:11, one launch (start us, length us, event | category | flops | bytes accessed | tf_op | source)
XLA Modules:
  0.0 374.4 jit_solution(9177522312073506477)
XLA Ops:
  8.6 2.0 fusion.10
  15.8 2.5 select_convert_fusion
  20.5 2.3 slice_bitcast_fusion.1
  22.7 3.7 fusion.16
  26.5 2.0 pad_maximum_fusion.2
  28.5 5.6 %gather_fusion = bf16[128,128,128]{2,1,0:T(8,128)(2,1)} fusion(bf16[160,128,128]{2,1,0:T(8,128)(2,1)} %param.20, s32[1024]{0:T(1024)S(1)} %get-tuple-element.62), kind=kCustom, calls=%fused_computation | custom fusion | bytes 8389120 | tf_op jit(solution)/shard_map/gather | solution.py:365
  34.1 5.5 %gather_fusion.1 = bf16[128,128,128]{2,1,0:T(8,128)(2,1)} fusion(bf16[160,128,128]{2,1,0:T(8,128)(2,1)} %param.21, s32[1024]{0:T(1024)S(1)} %get-tuple-element.62), kind=kCustom, calls=%fused_computation.1 | custom fusion | bytes 8389120 | tf_op jit(solution)/shard_map/gather | solution.py:366
  39.6 4.1 %gather_fusion.2 = bf16[32,128,128]{2,1,0:T(8,128)(2,1)} fusion(bf16[160,128,128]{2,1,0:T(8,128)(2,1)} %param.20, s32[1024]{0:T(1024)S(1)} %get-tuple-element.61), kind=kCustom, calls=%fused_computation.2 | custom fusion | bytes 2097280 | tf_op jit(solution)/shard_map/gather | solution.py:367
  43.7 4.1 %gather_fusion.3 = bf16[32,128,128]{2,1,0:T(8,128)(2,1)} fusion(bf16[160,128,128]{2,1,0:T(8,128)(2,1)} %param.21, s32[1024]{0:T(1024)S(1)} %get-tuple-element.61), kind=kCustom, calls=%fused_computation.3 | custom fusion | bytes 2097280 | tf_op jit(solution)/shard_map/gather | solution.py:368
  49.3 33.0 %all-gather.3.cloned.1.call-done.rows_ref = bf16[2048,2048]{1,0:T(8,128)(2,1)} async-done(((bf16[128,2048]{1,0:T(8,128)(2,1)}), bf16[2048,2048]{1,0:T(8,128)(2,1)}) %all-gather.3.cloned.1.call-update) | async-done | bytes 8388624 | tf_op jit(solution)/shard_map/all_gather | solution.py:407
  82.4 1.7 collective-permute-start.2
  84.1 28.8 %attend.1 = (bf16[2048,128]{1,0:T(8,128)(2,1)}, bf16[2,2048,128]{2,1,0:T(8,128)(2,1)}) custom-call(s32[4]{0:T(128)} %dec_len_ref.1, s32[1]{0:T(128)} %copy.28.pre_pos_ref, bf16[2048,2048]{1,0:T(8,128)(2,1)} %all-gather.3.cloned.1.call-done.rows_ref, bf16[2048,384]{1,0:T(8,128)(2,1)} %pad_maximum_fusion.weight_ref, f32[2048,128]{1,0:T(8,128)} %get-tuple-element.26.cos_ref, ...), custom_call_target="tpu_custom_call" | custom-call | flops 8589934592 | bytes 25165824 | tf_op jit(solution)/shard_map/attend/pallas_call | solution.py:202
  112.9 23.7 %all-gather.5.cloned.1.call-done = bf16[1024,2048]{1,0:T(8,128)(2,1)} async-done(((bf16[64,2048]{1,0:T(8,128)(2,1)}), bf16[1024,2048]{1,0:T(8,128)(2,1)}) %all-gather.5.cloned.1.call-update) | async-done | bytes 4194320 | tf_op jit(solution)/shard_map/all_gather | solution.py:422
  137.5 3.8 %slice_bitcast_fusion = bf16[1536,1024]{1,0:T(8,128)(2,1)} fusion(bf16[1,2048,1024]{2,1,0:T(8,128)(2,1)} %param.30), kind=kLoop, calls=%fused_computation.5 | loop fusion | bytes 6291456 | tf_op jit(solution)/shard_map/squeeze | solution.py:435
  141.3 11.7 %exchange.3 = bf16[16,128,128]{2,1,0:T(8,128)(2,1)} custom-call(bf16[16,128,128]{2,1,0:T(8,128)(2,1)} %bitcast.76), custom_call_target="tpu_custom_call" | custom-call | tf_op jit(solution)/shard_map/exchange/pallas_call | solution.py:278
  157.2 3.1 fusion.34
  161.5 2.4 collective-permute-start.4
  165.5 3.9 %convolution_convert_fusion = bf16[1280,2048]{1,0:T(8,128)(2,1)} fusion(bf16[1280,256]{1,0:T(8,128)(2,1)S(1)} %fusion.6, bf16[128,2048]{1,0:T(8,128)(2,1)S(1)} %collective-permute-done.4, bf16[128,2048]{1,0:T(8,128)(2,1)S(1)} %multiply_convert_fusion), kind=kOutput, calls=%fused_computation.4 | convolution fusion | flops 1346895872 | bytes 6946816 | tf_op jit(solution)/shard_map/dot_general | solution.py:450
  169.3 75.4 %exchange.4 = bf16[32,40,2048]{2,1,0:T(8,128)(2,1)} custom-call(bf16[32,40,2048]{2,1,0:T(8,128)(2,1)} %bitcast.65), custom_call_target="tpu_custom_call" | custom-call | tf_op jit(solution)/shard_map/exchange/pallas_call | solution.py:278
  244.7 21.8 %collective-permute-done.6.down_b_ref = bf16[512,2048]{1,0:T(8,128)(2,1)} collective-permute-done((bf16[512,2048]{1,0:T(8,128)(2,1)}, bf16[512,2048]{1,0:T(8,128)(2,1)}, u32[]{:S(2)}, u32[]{:S(2)}) %collective-permute-start.6) | collective-permute-done | bytes 2097184 | tf_op jit(solution)/shard_map/ppermute | solution.py:438
  266.5 23.5 %experts.1 = bf16[1280,2048]{1,0:T(8,128)(2,1)} custom-call(bf16[1280,2048]{1,0:T(8,128)(2,1)} %bitcast.67, bf16[2048,1024]{1,0:T(8,128)(2,1)} %bitcast.71, bf16[512,1024]{1,0:T(8,128)(2,1)} %copy-done.9, bf16[1536,1024]{1,0:T(8,128)(2,1)} %collective-permute-done.5.in_b1_ref, bf16[512,2048]{1,0:T(8,128)(2,1)} %bitcast.79, ...), custom_call_target="tpu_custom_call" | custom-call | flops 16106127360 | bytes 25165824 | tf_op jit(solution)/shard_map/experts/pallas_call | solution.py:314
  290.1 66.8 %exchange.5 = bf16[32,40,2048]{2,1,0:T(8,128)(2,1)} custom-call(bf16[32,40,2048]{2,1,0:T(8,128)(2,1)} %bitcast.68), custom_call_target="tpu_custom_call" | custom-call | tf_op jit(solution)/shard_map/exchange/pallas_call | solution.py:278
  356.9 4.8 %fusion.35 = f32[512,2048]{1,0:T(8,128)S(1)} fusion(bf16[512,1280]{0,1:T(8,128)(2,1)S(1)} %pad_maximum_fusion.1, bf16[1280,2048]{1,0:T(8,128)(2,1)} %bitcast.66), kind=kOutput, calls=%fused_computation.94 | convolution fusion | flops 2684354560 | bytes 10747904 | tf_op jit(solution)/shard_map/dot_general | solution.py:456
  362.2 2.8 collective-permute-start.7
  (74 shorter events, 20.1 us)
Async XLA Ops:
  7.2 11.1 %copy-start = (bf16[128,2048]{1,0:T(8,128)(2,1)S(1)}, bf16[128,2048]{1,0:T(8,128)(2,1)}, u32[]{:S(2)}) copy-start(bf16[128,2048]{1,0:T(8,128)(2,1)} %param.26) | copy-start | bytes 1572868
  7.2 11.8 %copy-start.5 = (bf16[2,2048,128]{2,1,0:T(8,128)(2,1)S(1)}, bf16[2,2048,128]{2,1,0:T(8,128)(2,1)}, u32[]{:S(2)}) copy-start(bf16[2,2048,128]{2,1,0:T(8,128)(2,1)} %param.19) | copy-start | bytes 3145732
  7.2 11.9 %copy-start.6 = (bf16[2048,128]{1,0:T(8,128)(2,1)S(1)}, bf16[2048,128]{1,0:T(8,128)(2,1)}, u32[]{:S(2)}) copy-start(bf16[2048,128]{1,0:T(8,128)(2,1)} %param.18) | copy-start | bytes 1572868
  7.2 75.1 %all-gather.3.cloned.1.call-start = ((), (), s32[]{:S(2)}) async-start(), calls=%async_computation | async-start | bytes 8912896 | tf_op jit(solution)/shard_map/all_gather | solution.py:407
  10.7 126.0 %all-gather.5.cloned.1.call-start = ((), (), s32[]{:S(2)}) async-start(), calls=%async_computation.1 | async-start | bytes 4456448 | tf_op jit(solution)/shard_map/all_gather | solution.py:422
  10.7 37.2 %collective-permute-start.1 = (f32[128,8]{0,1:T(8,128)}, f32[128,8]{0,1:T(8,128)S(1)}, u32[]{:S(2)}, u32[]{:S(2)}) collective-permute-start(f32[128,8]{0,1:T(8,128)} %param.29), channel_id=1, source_target_pairs={{0,16},{16,0},{32,48},{48,32},{64,80},{80,64},{96,112},{112,96},{1... | collective-permute-start | bytes 12296 | tf_op jit(solution)/shard_map/ppermute | solution.py:379
  11.5 36.5 %collective-permute-start = (s32[128,8]{0,1:T(8,128)}, s32[128,8]{0,1:T(8,128)S(1)}, u32[]{:S(2)}, u32[]{:S(2)}) collective-permute-start(s32[128,8]{0,1:T(8,128)} %param.28), channel_id=1, source_target_pairs={{0,16},{16,0},{32,48},{48,32},{64,80},{80,64},{96,112},{112,96},{1... | collective-permute-start | bytes 12296 | tf_op jit(solution)/shard_map/ppermute | solution.py:377
  39.6 8.4 %copy-start.8 = (s32[128,8]{0,1:T(8,128)S(1)}, s32[128,8]{0,1:T(8,128)}, u32[]{:S(2)}) copy-start(s32[128,8]{0,1:T(8,128)} %param.28) | copy-start | bytes 12292
  82.4 30.5 %collective-permute-start.2 = (bf16[512,1024]{1,0:T(8,128)(2,1)}, bf16[512,1024]{1,0:T(8,128)(2,1)S(1)}, u32[]{:S(2)}, u32[]{:S(2)}) collective-permute-start(bf16[512,1024]{1,0:T(8,128)(2,1)} %slice_bitcast_fusion.1), channel_id=1, source_target_pairs={{0,1},{1,0},{2,3},{3,2},{4,5},{5,4},{6,7},{7,6},{8,9},{9,8},{10,11... | collective-permute-start | bytes 3145736 | tf_op jit(solution)/shard_map/ppermute | solution.py:423
  112.9 28.4 %copy-start.9 = (bf16[512,1024]{1,0:T(8,128)(2,1)}, bf16[512,1024]{1,0:T(8,128)(2,1)S(1)}, u32[]{:S(2)}) copy-start(bf16[512,1024]{1,0:T(8,128)(2,1)S(1)} %collective-permute-done.2.in_b0_ref) | copy-start | bytes 3145732
  136.6 20.6 %collective-permute-start.3 = (bf16[1024,2048]{1,0:T(8,128)(2,1)}, bf16[1024,2048]{1,0:T(8,128)(2,1)}, u32[]{:S(2)}, u32[]{:S(2)}) collective-permute-start(bf16[1024,2048]{1,0:T(8,128)(2,1)} %all-gather.5.cloned.1.call-done), channel_id=1, source_target_pairs={{0,16},{16,0},{32,48},{48,32},{64,80},{80,64},{96,112},{112,96},{1... | collective-permute-start | bytes 12582920 | tf_op jit(solution)/shard_map/ppermute | solution.py:430
  153.0 113.5 %collective-permute-start.5 = (bf16[1536,1024]{1,0:T(8,128)(2,1)}, bf16[1536,1024]{1,0:T(8,128)(2,1)}, u32[]{:S(2)}, u32[]{:S(2)}) collective-permute-start(bf16[1536,1024]{1,0:T(8,128)(2,1)} %slice_bitcast_fusion), channel_id=1, source_target_pairs={{0,1},{1,0},{2,3},{3,2},{4,5},{5,4},{6,7},{7,6},{8,9},{9,8},{10,11... | collective-permute-start | bytes 9437192 | tf_op jit(solution)/shard_map/ppermute | solution.py:437
  156.0 4.3 %copy-start.2 = (bf16[128,2048]{1,0:T(8,128)(2,1)S(1)}, bf16[128,2048]{1,0:T(8,128)(2,1)}, u32[]{:S(2)}) copy-start(bf16[128,2048]{1,0:T(8,128)(2,1)} %param.16) | copy-start | bytes 1572868
  156.9 3.5 copy-start.3
  156.9 3.5 copy-start.4
  156.9 109.6 %collective-permute-start.6 = (bf16[512,2048]{1,0:T(8,128)(2,1)}, bf16[512,2048]{1,0:T(8,128)(2,1)}, u32[]{:S(2)}, u32[]{:S(2)}) collective-permute-start(bf16[512,2048]{1,0:T(8,128)(2,1)} %bitcast.78), channel_id=1, source_target_pairs={{0,1},{1,0},{2,3},{3,2},{4,5},{5,4},{6,7},{7,6},{8,9},{9,8},{10,11... | collective-permute-start | bytes 6291464 | tf_op jit(solution)/shard_map/ppermute | solution.py:438
  160.4 0.9 copy-start.7
  161.5 4.0 %collective-permute-start.4 = (bf16[128,2048]{1,0:T(8,128)(2,1)S(1)}, bf16[128,2048]{1,0:T(8,128)(2,1)S(1)}, u32[]{:S(2)}, u32[]{:S(2)}) collective-permute-start(bf16[128,2048]{1,0:T(8,128)(2,1)S(1)} %multiply_convert_fusion), channel_id=1, source_target_pairs={{0,16},{16,0},{32,48},{48,32},{64,80},{80,64},{96,112},{112,96},{1... | collective-permute-start | bytes 1572872 | tf_op jit(solution)/shard_map/ppermute | solution.py:449
  361.8 5.8 %copy-start.1 = (bf16[128,2048]{1,0:T(8,128)(2,1)S(1)}, bf16[128,2048]{1,0:T(8,128)(2,1)}, u32[]{:S(2)}) copy-start(bf16[128,2048]{1,0:T(8,128)(2,1)} %param.26) | copy-start | bytes 1572868
  362.2 4.3 %collective-permute-start.7 = (bf16[128,2048]{1,0:T(8,128)(2,1)S(1)}, bf16[128,2048]{1,0:T(8,128)(2,1)S(1)}, u32[]{:S(2)}, u32[]{:S(2)}) collective-permute-start(bf16[128,2048]{1,0:T(8,128)(2,1)S(1)} %slice.85), channel_id=1, source_target_pairs={{0,16},{16,0},{32,48},{48,32},{64,80},{80,64},{96,112},{112,96},{1... | collective-permute-start | bytes 1572872 | tf_op jit(solution)/shard_map/ppermute | solution.py:460
Sparse Core Ops, SparseCore 0:
  10.8 71.4 all-gather.2
  84.5 52.1 all-gather.4
